TPU v7x, 32 devices: a whole 2x2x4 slice. The times are simulated.
32 devices in a mesh: doc: 8 (over z, y), term: 4 (over x, core).
Axes of the slice: x: 2, y: 2, z: 4, core: 2. Of those that a mesh axis runs over, the one named last changes fastest.
Arguments:
- tfidf: bfloat16 [4096, 8192], P('term', 'doc'), may hold values from 50 to 1000
- pattern: int32 [32, 64], P('term', 'doc'), may hold values 0 or 1
- factor_w: bfloat16 [4096, 256], P('term'), may hold values from 0.29882812 to 3
- factor_h: bfloat16 [256, 8192], P(None, 'doc'), may hold values from 0.29882812 to 3
Outputs:
- updated_w: bfloat16 [4096, 256], P('term')
- updated_h: bfloat16 [256, 8192], P(None, 'doc')
All inputs are finite; a program needn't handle non-finite values. No bound on the sum of `pattern` on one device may be relied on, other than what follows from the above.
Results may differ from a plain program's by a relative error of at most 0.0004.
The roundings to bfloat16 on the way count: a program that leaves them out, or rounds other values in their place, can miss the bound.
Values may be sent and summed in bfloat16 or wider, within the bound.
No kernel may reach another device: no remote copies, remote signals or barrier semaphores. Data moves between devices by JAX's collectives and lax.ppermute only.
A program may use at most 64 MiB of HBM per device.

v0:
```python
import jax
import jax.numpy as jnp
from jax import lax
from jax.sharding import PartitionSpec as P

BLOCK = 128


def expand(pattern):
    block_rows, block_cols = pattern.shape
    spread = jnp.broadcast_to(pattern[:, None, :, None], (block_rows, BLOCK, block_cols, BLOCK))
    return spread.reshape(block_rows * BLOCK, block_cols * BLOCK)


def contract_first(operand_one, operand_two):
    return lax.dot_general(
        operand_one, operand_two, (((0,), (0,)), ((), ())), preferred_element_type=jnp.float32
    )


def contract_last(operand_one, operand_two):
    return lax.dot_general(
        operand_one, operand_two, (((1,), (1,)), ((), ())), preferred_element_type=jnp.float32
    )


def on_device(tfidf, pattern, factor_w, factor_h):
    masked = tfidf * expand(pattern).astype(jnp.bfloat16)
    gram_part = contract_first(factor_w, factor_w)
    numer_part = contract_first(factor_w, masked)
    gram_w = lax.psum(gram_part, "term")
    numerator = lax.psum_scatter(numer_part, "term", scatter_dimension=1, tiled=True)
    share_width = numerator.shape[1]
    old_share = lax.dynamic_slice_in_dim(
        factor_h, lax.axis_index("term") * share_width, share_width, 1
    )
    denominator = jnp.dot(
        gram_w.astype(jnp.bfloat16), old_share, preferred_element_type=jnp.float32
    )
    h_part = (old_share.astype(jnp.float32) * numerator / denominator).astype(jnp.bfloat16)
    new_h = lax.all_gather(h_part, "term", axis=1, tiled=True)
    gram_h_part = contract_last(new_h, new_h)
    term_topic, gram_h = lax.psum((contract_last(masked, new_h), gram_h_part), "doc")
    denominator = jnp.dot(factor_w, gram_h.astype(jnp.bfloat16), preferred_element_type=jnp.float32)
    new_w = (factor_w.astype(jnp.float32) * term_topic / denominator).astype(jnp.bfloat16)
    return (new_w, new_h)


def solution(mesh):
    placed = (P("term", "doc"), P("term", "doc"), P("term", None), P(None, "doc"))
    return jax.shard_map(
        on_device,
        mesh=mesh,
        in_specs=placed,
        out_specs=(P("term", None), P(None, "doc")),
        check_vma=False,
    )
```

profile of v0, /device:TPU:0, one launch (start us, length us, event | category | flops | bytes accessed | tf_op | source)
XLA Modules:
  0.0 143.6 jit_solution(14670027527547338195)
XLA Ops:
  7.2 0.0 copy-start
  7.2 0.0 copy-start.1
  7.2 0.0 reduce-scatter.2.cloned.1.call-start
  7.2 0.8 convert_element_type.26
  8.0 0.3 broadcast_in_dim.2
  8.4 0.0 copy-start.2
  8.4 1.3 copy-done.2
  9.7 0.0 copy-done.1
  9.7 3.5 %convolution_bitcast_fusion = f32[256,1024]{0,1:T(8,128)} fusion(bf16[1024,256]{1,0:T(8,128)(2,1)S(1)} %copy-done.1, bf16[1024,1024]{1,0:T(8,128)(2,1)} %param.4, bf16[128,8,8,128]{3,2,1,0:T(8,128)(2,1)S(1)} %bitcast.24), kind=kOutput, calls=%fused_computation.1 | convolution fusion | flops 537919488 | bytes 5767168 | tf_op jit(solution)/shard_map/dot_general | solution.py:16
  13.2 0.0 reduce-scatter.2.cloned.1.call-update
  13.3 0.0 all-reduce.4.cloned.1.call-start
  13.3 0.0 copy-done
  13.4 0.1 copy.12
  13.5 0.3 fusion.6
  13.8 16.3 %all-reduce.5 = bf16[256,256]{1,0:T(8,128)(2,1)S(1)} all-reduce(f32[256,256]{1,0:T(8,128)S(1)} %fusion.6), channel_id=1, replica_groups=mesh['doc'=8,'term'=4] {'term'}, use_global_device_ids=true, to_apply=%region_1.0 | all-reduce | flops 65536 | bytes 393216 | tf_op jit(solution)/shard_map/psum | solution.py:31
  30.1 10.8 %reduce-scatter.2.cloned.1.call-done = f32[256,256]{0,1:T(8,128)} async-done(((f32[256,1024]{0,1:T(8,128)}), f32[256,256]{0,1:T(8,128)}) %reduce-scatter.2.cloned.1.call-update) | async-done | bytes 262160 | tf_op jit(solution)/shard_map/reduce_scatter | solution.py:32
  40.9 1.2 fusion.2
  42.1 6.6 %all_gather.3 = bf16[256,1024]{0,1:T(8,128)(2,1)S(1)} all-gather(bf16[256,256]{0,1:T(8,128)(2,1)S(1)} %fusion.2), channel_id=1, replica_groups=mesh['doc'=8,'term'=4] {'term'}, dimensions={1}, use_global_device_ids=true | all-gather | bytes 655360 | tf_op jit(solution)/shard_map/all_gather | solution.py:41
  48.7 3.9 %fusion.3 = f32[1024,256]{1,0:T(8,128)} fusion(bf16[256,1024]{0,1:T(8,128)(2,1)S(1)} %all_gather.3, bf16[1024,1024]{1,0:T(8,128)(2,1)} %param.4, bf16[128,8,8,128]{3,2,1,0:T(8,128)(2,1)} %bitcast.25), kind=kOutput, calls=%fused_computation.7 | convolution fusion | flops 537919488 | bytes 5767168 | tf_op jit(solution)/shard_map/dot_general | solution.py:22
  52.6 0.0 all-reduce.4.cloned.1.call-update
  52.6 1.0 copy.9
  53.6 0.3 fusion.7
  54.0 41.6 %all-reduce.6 = bf16[256,256]{1,0:T(8,128)(2,1)S(1)} all-reduce(f32[256,256]{1,0:T(8,128)S(1)} %fusion.7), channel_id=1, replica_groups=mesh['doc'=8,'term'=4] {'doc'}, use_global_device_ids=true, to_apply=%region_3.0 | all-reduce | flops 65536 | bytes 393216 | tf_op jit(solution)/shard_map/psum | solution.py:43
  95.6 38.9 %all-reduce.4.cloned.1.call-done = f32[1024,256]{1,0:T(8,128)} async-done(((f32[1024,256]{1,0:T(8,128)}), f32[1024,256]{1,0:T(8,128)}) %all-reduce.4.cloned.1.call-update) | async-done | bytes 1048592 | tf_op jit(solution)/shard_map/psum | solution.py:43
  134.5 2.3 %fusion.1 = bf16[1024,256]{1,0:T(8,128)(2,1)} fusion(bf16[1024,256]{1,0:T(8,128)(2,1)S(1)} %copy-done.1, f32[1024,256]{1,0:T(8,128)} %all-reduce.4.cloned.1.call-done, bf16[256,256]{1,0:T(8,128)(2,1)S(1)} %all-reduce.6), kind=kOutput, calls=%fused_computation.4 | convolution fusion | flops 135266304 | bytes 2228224 | tf_op jit(solution)/shard_map/dot_general | solution.py:44
  (1 shorter events, 0.0 us)
Async XLA Ops:
  7.2 6.2 %copy-start = (bf16[256,1024]{1,0:T(8,128)(2,1)S(1)}, bf16[256,1024]{1,0:T(8,128)(2,1)}, u32[]{:S(2)}) copy-start(bf16[256,1024]{1,0:T(8,128)(2,1)} %param.7) | copy-start | bytes 1572868
  7.2 2.5 %copy-start.1 = (bf16[1024,256]{1,0:T(8,128)(2,1)S(1)}, bf16[1024,256]{1,0:T(8,128)(2,1)}, u32[]{:S(2)}) copy-start(bf16[1024,256]{1,0:T(8,128)(2,1)} %param.6) | copy-start | bytes 1572868
  7.2 33.7 %reduce-scatter.2.cloned.1.call-start = ((), (), s32[]{:S(2)}) async-start(), calls=%async_computation.1 | async-start | bytes 1310720 | tf_op jit(solution)/shard_map/reduce_scatter | solution.py:32
  8.4 1.4 copy-start.2
  13.3 121.2 %all-reduce.4.cloned.1.call-start = ((), (), s32[]{:S(2)}) async-start(), calls=%async_computation.2 | async-start | bytes 2097152 | tf_op jit(solution)/shard_map/psum | solution.py:43
Sparse Core Ops, SparseCore 0:
  13.4 27.4 reduce-scatter.1
  52.8 81.6 all-reduce.3
where the time goes:
time: 144 us
  blocking collectives  64.4 us (45%)
  waiting for transfers between devices  49.8 us (35%)
  between operations  14.1 us (10%)
  matrix products  11.6 us (8%)
  local copies, waits for them, and re-layouts  2.82 us (2%)
    psum x1, blocking collectives, on_device(): lax.psum((contract_last(masked, new_h), gram_h_part), 'doc')  41.6 us
    psum x1, waiting for transfers between devices, on_device(): lax.psum((contract_last(masked, new_h), gram_h_part), 'doc')  38.9 us
    psum x1, blocking collectives, on_device(): gram_w = lax.psum(gram_part, 'term')  16.3 us
    reduce_scatter x1, waiting for transfers between devices, on_device(): lax.psum_scatter(numer_part, 'term', scatter_dimension=1, tiled=True)  10.8 us
    all_gather x1, blocking collectives, on_device(): new_h = lax.all_gather(h_part, 'term', axis=1, tiled=True)  6.58 us
    dot_general x2, matrix products, contract_last(): lax.dot_general(operand_one, operand_two, (((1,), (1,)), ((), ())), prefe...  4.26 us
    dot_general x2, matrix products, contract_first(): lax.dot_general(operand_one, operand_two, (((0,), (0,)), ((), ())), prefe...  3.86 us
  transfers between devices with their start and end apart: 2, of which 2 were waited for; matrix products, arithmetic and copies ran while one was open for 1% of the time, Pallas kernels for 0%

commit v1 on v0

--- a/solution.py
+++ b/solution.py
@@ -28,7 +28,8 @@
     masked = tfidf * expand(pattern).astype(jnp.bfloat16)
     gram_part = contract_first(factor_w, factor_w)
     numer_part = contract_first(factor_w, masked)
-    gram_w = lax.psum(gram_part, "term")
+    parts = lax.all_gather(gram_part, "term")
+    gram_w = jnp.sum(parts, axis=0)
     numerator = lax.psum_scatter(numer_part, "term", scatter_dimension=1, tiled=True)
     share_width = numerator.shape[1]
     old_share = lax.dynamic_slice_in_dim(

time: 144 us -> 160 us (1.11)
  waiting for transfers between devices: 49.8 us -> 80.3 us
  blocking collectives: 64.4 us -> 48.2 us
    psum x1 -> x0, blocking collectives: 16.3 us -> none  [on_device(): gram_w = lax.psum(gram_part, 'term')]
    all_gather x0 -> x1, waiting for transfers between devices: none -> 15.3 us  [on_device(): parts = lax.all_gather(gram_part, 'term')]
    reduce_scatter x1, waiting for transfers between devices: 10.8 us -> 26 us  [on_device(): lax.psum_scatter(numer_part, 'term', scatter_dimension=1, tiled=True)]
  transfers between devices with their start and end apart: 2 -> 3, of which waited for: 2 -> 3; matrix products, arithmetic and copies ran while one was open for 1% -> 4% of each run, Pallas kernels for 0% -> 0%
where the time goes in v1:
time: 160 us; the launch traced here: 159 us
  waiting for transfers between devices  80.3 us (50%)
  blocking collectives  48.2 us (30%)
  between operations  13.8 us (9%)
  matrix products  12.1 us (8%)
  local copies, waits for them, and re-layouts  2.82 us (2%)
  other arithmetic  1.99 us (1%)
    psum x1, blocking collectives, on_device(): lax.psum((contract_last(masked, new_h), gram_h_part), 'doc')  41.6 us
    psum x1, waiting for transfers between devices, on_device(): lax.psum((contract_last(masked, new_h), gram_h_part), 'doc')  38.9 us
    reduce_scatter x1, waiting for transfers between devices, on_device(): lax.psum_scatter(numer_part, 'term', scatter_dimension=1, tiled=True)  26 us
    all_gather x1, waiting for transfers between devices, on_device(): parts = lax.all_gather(gram_part, 'term')  15.3 us
    all_gather x1, blocking collectives, on_device(): new_h = lax.all_gather(h_part, 'term', axis=1, tiled=True)  6.6 us
    dot_general x2, matrix products, contract_first(): lax.dot_general(operand_one, operand_two, (((0,), (0,)), ((), ())), prefe...  4.33 us
    dot_general x2, matrix products, contract_last(): lax.dot_general(operand_one, operand_two, (((1,), (1,)), ((), ())), prefe...  4.26 us
  transfers between devices with their start and end apart: 3, of which 3 were waited for; matrix products, arithmetic and copies ran while one was open for 4% of the time, Pallas kernels for 0%

profile of v1, /device:TPU:0, one launch (start us, length us, event | category | flops | bytes accessed | tf_op | source)
XLA Modules:
  0.0 159.4 jit_solution(15695729897140126332)
XLA Ops:
  7.2 0.0 copy-start
  7.2 0.0 copy-start.1
  7.2 0.0 copy-start.3
  7.2 0.0 all-gather.3.cloned.1.call-start
  7.2 2.4 %fusion.6 = f32[256,256]{1,0:T(8,128)} fusion(bf16[1024,256]{1,0:T(8,128)(2,1)} %param.6), kind=kOutput, calls=%fused_computation.11 | convolution fusion | flops 134217728 | bytes 786432 | tf_op jit(solution)/shard_map/dot_general | solution.py:16
  9.6 0.0 all-gather.3.cloned.1.call-update
  9.7 0.0 reduce-scatter.2.cloned.1.call-start
  9.7 0.7 convert_element_type.26
  10.4 0.3 broadcast_in_dim.2
  10.7 0.0 copy-start.2
  10.8 1.3 copy-done.2
  12.1 0.0 copy-done.1
  12.1 0.0 copy-done.3
  12.1 1.9 %convolution_bitcast_fusion = f32[256,1024]{0,1:T(8,128)} fusion(bf16[1024,256]{1,0:T(8,128)(2,1)S(1)} %copy-done.1, bf16[1024,1024]{1,0:T(8,128)(2,1)S(1)} %copy-done.3, bf16[128,8,8,128]{3,2,1,0:T(8,128)(2,1)S(1)} %bitcast.25), kind=kOutput, calls=%fused_computation.1 | convolution fusion | flops 537919488 | bytes 5767168 | tf_op jit(solution)/shard_map/dot_general | solution.py:16
  14.0 0.0 reduce-scatter.2.cloned.1.call-update
  14.1 0.0 all-reduce.3.cloned.1.call-start
  14.1 0.0 copy-done
  14.2 0.1 copy.12
  14.3 15.3 %all-gather.3.cloned.1.call-done = f32[1024,256]{1,0:T(8,128)} async-done(((f32[256,256]{1,0:T(8,128)}), f32[1024,256]{1,0:T(8,128)}) %all-gather.3.cloned.1.call-update) | async-done | bytes 1048592 | tf_op jit(solution)/shard_map/all_gather | solution.py:31
  29.6 1.3 reduce_sum.9
  30.9 26.0 %reduce-scatter.2.cloned.1.call-done = f32[256,256]{0,1:T(8,128)} async-done(((f32[256,1024]{0,1:T(8,128)}), f32[256,256]{0,1:T(8,128)}) %reduce-scatter.2.cloned.1.call-update) | async-done | bytes 262160 | tf_op jit(solution)/shard_map/reduce_scatter | solution.py:33
  56.9 1.2 fusion.2
  58.1 6.6 %all_gather.11 = bf16[256,1024]{0,1:T(8,128)(2,1)S(1)} all-gather(bf16[256,256]{0,1:T(8,128)(2,1)S(1)} %fusion.2), channel_id=1, replica_groups=mesh['doc'=8,'term'=4] {'term'}, dimensions={1}, use_global_device_ids=true | all-gather | bytes 655360 | tf_op jit(solution)/shard_map/all_gather | solution.py:42
  64.7 3.9 %fusion.3 = f32[1024,256]{1,0:T(8,128)} fusion(bf16[256,1024]{0,1:T(8,128)(2,1)S(1)} %all_gather.11, bf16[1024,1024]{1,0:T(8,128)(2,1)} %param.4, bf16[128,8,8,128]{3,2,1,0:T(8,128)(2,1)} %bitcast.26), kind=kOutput, calls=%fused_computation.7 | convolution fusion | flops 537919488 | bytes 5767168 | tf_op jit(solution)/shard_map/dot_general | solution.py:22
  68.7 0.0 all-reduce.3.cloned.1.call-update
  68.7 1.0 copy.9
  69.7 0.3 fusion.7
  70.0 41.6 %all-reduce.4 = bf16[256,256]{1,0:T(8,128)(2,1)S(1)} all-reduce(f32[256,256]{1,0:T(8,128)S(1)} %fusion.7), channel_id=1, replica_groups=mesh['doc'=8,'term'=4] {'doc'}, use_global_device_ids=true, to_apply=%region_3.0 | all-reduce | flops 65536 | bytes 393216 | tf_op jit(solution)/shard_map/psum | solution.py:44
  111.6 38.9 %all-reduce.3.cloned.1.call-done = f32[1024,256]{1,0:T(8,128)} async-done(((f32[1024,256]{1,0:T(8,128)}), f32[1024,256]{1,0:T(8,128)}) %all-reduce.3.cloned.1.call-update) | async-done | bytes 1048592 | tf_op jit(solution)/shard_map/psum | solution.py:44
  150.5 2.3 %fusion.1 = bf16[1024,256]{1,0:T(8,128)(2,1)} fusion(bf16[1024,256]{1,0:T(8,128)(2,1)S(1)} %copy-done.1, f32[1024,256]{1,0:T(8,128)} %all-reduce.3.cloned.1.call-done, bf16[256,256]{1,0:T(8,128)(2,1)S(1)} %all-reduce.4), kind=kOutput, calls=%fused_computation.4 | convolution fusion | flops 135266304 | bytes 2228224 | tf_op jit(solution)/shard_map/dot_general | solution.py:45
  (1 shorter events, 0.0 us)
Async XLA Ops:
  7.2 7.0 %copy-start = (bf16[256,1024]{1,0:T(8,128)(2,1)S(1)}, bf16[256,1024]{1,0:T(8,128)(2,1)}, u32[]{:S(2)}) copy-start(bf16[256,1024]{1,0:T(8,128)(2,1)} %param.7) | copy-start | bytes 1572868
  7.2 4.9 %copy-start.1 = (bf16[1024,256]{1,0:T(8,128)(2,1)S(1)}, bf16[1024,256]{1,0:T(8,128)(2,1)}, u32[]{:S(2)}) copy-start(bf16[1024,256]{1,0:T(8,128)(2,1)} %param.6) | copy-start | bytes 1572868
  7.2 4.9 %copy-start.3 = (bf16[1024,1024]{1,0:T(8,128)(2,1)S(1)}, bf16[1024,1024]{1,0:T(8,128)(2,1)}, u32[]{:S(2)}) copy-start(bf16[1024,1024]{1,0:T(8,128)(2,1)} %param.4) | copy-start | bytes 6291460
  7.2 22.4 %all-gather.3.cloned.1.call-start = ((), (), s32[]{:S(2)}) async-start(), calls=%async_computation.3 | async-start | bytes 1310720 | tf_op jit(solution)/shard_map/all_gather | solution.py:31
  9.7 47.3 %reduce-scatter.2.cloned.1.call-start = ((), (), s32[]{:S(2)}) async-start(), calls=%async_computation.1 | async-start | bytes 1310720 | tf_op jit(solution)/shard_map/reduce_scatter | solution.py:33
  10.7 1.3 copy-start.2
  14.1 136.5 %all-reduce.3.cloned.1.call-start = ((), (), s32[]{:S(2)}) async-start(), calls=%async_computation.2 | async-start | bytes 2097152 | tf_op jit(solution)/shard_map/psum | solution.py:44
Sparse Core Ops, SparseCore 0:
  10.1 19.4 all-gather.2
  32.1 24.7 reduce-scatter.1
  68.8 81.6 all-reduce.2
